TPU v7x, 256 devices: a whole 4x4x8 slice. The times are simulated.
256 devices in a mesh: dp: 2 (over z_lo), node: 16 (over x, z_hi), local: 8 (over y, core).
Axes of the slice: x: 4, y: 4, z: 8 (z_hi: 4, z_lo: 2; z = z_hi * 2 + z_lo), core: 2. Of those that a mesh axis runs over, the one named last changes fastest.
Arguments:
- tokens_in: bfloat16 [2, 16, 64, 16, 3584], P('dp', 'node'), may hold values from -6 to 6
- grad_rows: bfloat16 [2, 16, 64, 16, 3584], P('dp', 'node'), may hold values from -6 to 6
- combine_weights: float32 [2, 16, 64, 16], P('dp', 'node'), may hold values from 0.05 to 1
- live_counts: int32 [2, 16, 16], P('dp', 'node'), may hold values from 0 to 64, as said below
- w_gate: bfloat16 [16, 3584, 2048], P('node', None, 'local'), may hold values from -0.09375 to 0.09375
- w_up: bfloat16 [16, 3584, 2048], P('node', None, 'local'), may hold values from -0.09375 to 0.09375
- w_down: bfloat16 [16, 3584, 2048], P('node', None, 'local'), may hold values from -0.125 to 0.125
Outputs:
- d_tokens: bfloat16 [2, 16, 64, 16, 3584], P('dp', 'node', 'local')
- grad_gate: bfloat16 [16, 3584, 2048], P('node', 'dp', 'local')
- grad_up: bfloat16 [16, 3584, 2048], P('node', 'dp', 'local')
- grad_down: bfloat16 [16, 3584, 2048], P('node', 'dp', 'local')
Inputs may be any that keep to these rules, and one draw needn't show every extreme that they name: `live_counts`: each replica has some source and expert pair with all 64 slots live; loads differ strongly between experts.
All inputs are finite; a program needn't handle non-finite values.
Results may differ from a plain program's by a relative error of at most 0.019.
Values may be sent and summed in bfloat16 or wider, within the bound.
A program may use at most 128 MiB of HBM per device.

v0:
```python
import jax
import jax.numpy as jnp
from jax import lax
from jax.sharding import PartitionSpec as P


def on_device(tokens_in, grad_rows, combine_weights, live_counts, w_gate, w_up, w_down):
    slot_count = tokens_in.shape[2]
    node_count = tokens_in.shape[3]
    feature_width = tokens_in.shape[4]
    gate_weight = w_gate[0]
    up_weight = w_up[0]
    down_weight = w_down[0]
    hid_local = gate_weight.shape[1]
    live_mask = (
        lax.broadcasted_iota(jnp.int32, (slot_count, node_count), 0) < live_counts[0, 0][None, :]
    ).astype(jnp.float32)
    scaled_rows = (
        grad_rows[0, 0].astype(jnp.float32) * (combine_weights[0, 0] * live_mask)[:, :, None]
    ).astype(jnp.bfloat16)
    scaled_rows = scaled_rows.reshape(slot_count * node_count, feature_width)
    flat_tokens = tokens_in[0, 0].reshape(slot_count * node_count, feature_width)
    gate_pre = jnp.dot(flat_tokens, gate_weight, preferred_element_type=jnp.float32)
    up_pre = jnp.dot(flat_tokens, up_weight, preferred_element_type=jnp.float32)
    sigmoid_gate = jax.nn.sigmoid(gate_pre)
    activated = gate_pre * sigmoid_gate
    hidden = (activated * up_pre).astype(jnp.bfloat16)
    hidden_grad = jnp.dot(scaled_rows, down_weight, preferred_element_type=jnp.float32)
    gate_grad = (
        hidden_grad * up_pre * sigmoid_gate * (1.0 + gate_pre * (1.0 - sigmoid_gate))
    ).astype(jnp.bfloat16)
    up_grad = (hidden_grad * activated).astype(jnp.bfloat16)
    joined_grad = jnp.concatenate((gate_grad, up_grad), axis=1)
    keep_rows = slot_count // lax.axis_size("local")
    total = lax.dot_general(
        gate_grad, gate_weight, (((1,), (1,)), ((), ())), preferred_element_type=jnp.float32
    )
    total = total + lax.dot_general(
        up_grad, up_weight, (((1,), (1,)), ((), ())), preferred_element_type=jnp.float32
    )
    summed = lax.psum_scatter(
        total.reshape(lax.axis_size("local") * keep_rows, node_count, feature_width).astype(
            jnp.bfloat16
        ),
        "local",
        scatter_dimension=0,
        tiled=True,
    )
    returned = lax.all_to_all(summed, "node", split_axis=1, concat_axis=1, tiled=True)
    d_tokens = returned[None, None]
    front = lax.dot_general(
        flat_tokens, joined_grad, (((0,), (0,)), ((), ())), preferred_element_type=jnp.float32
    )
    behind = lax.dot_general(
        scaled_rows, hidden, (((0,), (0,)), ((), ())), preferred_element_type=jnp.float32
    )
    weight_sums = lax.psum_scatter(
        jnp.concatenate((front, behind), axis=1).astype(jnp.bfloat16),
        "dp",
        scatter_dimension=0,
        tiled=True,
    ).astype(jnp.float32)
    grad_gate = weight_sums[:, :hid_local].astype(jnp.bfloat16)[None]
    grad_up = weight_sums[:, hid_local : 2 * hid_local].astype(jnp.bfloat16)[None]
    grad_down = weight_sums[:, 2 * hid_local :].astype(jnp.bfloat16)[None]
    return (d_tokens, grad_gate, grad_up, grad_down)


def solution(mesh):
    return jax.shard_map(
        on_device,
        mesh=mesh,
        in_specs=(
            P("dp", "node", None, None, None),
            P("dp", "node", None, None, None),
            P("dp", "node", None, None),
            P("dp", "node", None),
            P("node", None, "local"),
            P("node", None, "local"),
            P("node", None, "local"),
        ),
        out_specs=(
            P("dp", "node", "local", None, None),
            P("node", "dp", "local"),
            P("node", "dp", "local"),
            P("node", "dp", "local"),
        ),
        check_vma=False,
    )
```

profile of v0, /device:TPU:1, one launch (start us, length us, event | category | flops | bytes accessed | tf_op | source)
XLA Modules:
  0.0 213.1 jit_solution(1930631063470694649)
XLA Ops:
  7.2 0.0 copy-start
  7.2 0.0 reduce-scatter.7.cloned.1.call-start
  7.2 1.4 copy-done
  8.7 0.0 copy-start.2
  8.7 0.0 copy-start.6
  8.7 6.3 %fusion.4 = f32[1024,256]{0,1:T(8,128)} fusion(bf16[1024,3584]{1,0:T(8,128)(2,1)} %bitcast.56, bf16[1,3584,256]{2,1,0:T(8,128)(2,1)S(1)} %copy-done), kind=kOutput, calls=%fused_computation.10 | convolution fusion | flops 1879048192 | bytes 10223616 | tf_op jit(solution)/shard_map/dot_general | solution.py:23
  15.0 0.0 copy-done.2
  15.0 0.0 copy-done.6
  15.0 0.0 copy-start.4
  15.0 0.0 copy-start.5
  15.0 3.1 %fusion.7 = f32[1024,256]{0,1:T(8,128)} fusion(bf16[1024,3584]{1,0:T(8,128)(2,1)S(1)} %bitcast.58, bf16[1,3584,256]{2,1,0:T(8,128)(2,1)S(1)} %copy-done.2), kind=kOutput, calls=%fused_computation.13 | convolution fusion | flops 1879048192 | bytes 10223616 | tf_op jit(solution)/shard_map/dot_general | solution.py:24
  18.1 0.0 copy-done.4
  18.1 0.0 copy-done.5
  18.1 0.1 bitcast_select_fusion
  18.2 0.1 copy.27
  18.2 5.6 %multiply_convert_fusion = bf16[1,1,64,16,3584]{4,3,2,1,0:T(8,128)(2,1)S(1)} fusion(f32[64,16]{1,0:T(8,128)S(1)} %copy.27, bf16[1,1,64,16,3584]{4,3,2,1,0:T(8,128)(2,1)} %param.8), kind=kLoop, calls=%fused_computation.3 | loop fusion | flops 11010048 | bytes 14684160 | tf_op jit(solution)/shard_map/convert_element_type | solution.py:20
  23.8 4.5 %multiply_convert_fusion.2 = (bf16[1024,256]{0,1:T(8,128)(2,1)S(1)}, bf16[1024,256]{0,1:T(8,128)(2,1)S(1)}) fusion(f32[1024,256]{0,1:T(8,128)} %fusion.4, f32[1024,256]{0,1:T(8,128)} %fusion.7, bf16[1024,3584]{1,0:T(8,128)(2,1)S(1)} %bitcast.51, bf16[1,3584,256]{2,1,0:T(8,128)(2,1)} %param.13), kind=kOutput, calls=%fused_computation.21 | convolution fusion | flops 1882456064 | bytes 12320768 | tf_op jit(solution)/shard_map/dot_general | solution.py:28
  28.3 0.0 copy-start.3
  28.4 7.3 %fusion.2 = f32[1024,3584]{1,0:T(8,128)} fusion(bf16[1024,256]{0,1:T(8,128)(2,1)S(1)} %get-tuple-element.24, bf16[1,3584,256]{2,1,0:T(8,128)(2,1)S(1)} %copy-done), kind=kOutput, calls=%fused_computation.8 | convolution fusion | flops 1879048192 | bytes 17039360 | tf_op jit(solution)/shard_map/dot_general | solution.py:35
  35.7 0.0 copy-done.3
  35.7 7.5 %add_convert_fusion = bf16[1024,3584]{1,0:T(8,128)(2,1)S(1)} fusion(f32[1024,3584]{1,0:T(8,128)} %fusion.2, bf16[1024,256]{0,1:T(8,128)(2,1)S(1)} %get-tuple-element.23, bf16[1,3584,256]{2,1,0:T(8,128)(2,1)S(1)} %copy-done.3), kind=kOutput, calls=%fused_computation.2 | convolution fusion | flops 1886388224 | bytes 24379392 | tf_op jit(solution)/shard_map/dot_general | solution.py:38
  43.2 7.1 %copy.36 = bf16[8,8,16,3584]{3,1,2,0:T(8,128)(2,1)} copy(bf16[8,8,16,3584]{3,2,1,0:T(8,128)(2,1)S(1)} %bitcast.50) | data formatting | bytes 14680064
  50.4 0.0 reduce-scatter.7.cloned.1.call-update
  50.4 0.0 reduce-scatter.5.cloned.1.call-start
  50.4 0.1 copy.29
  50.5 0.1 squeeze.19
  50.6 0.1 iota.15
  50.7 0.1 lt.25
  50.8 5.5 %fusion = bf16[1024,3584]{1,0:T(8,128)(2,1)S(1)} fusion(f32[1024]{0:T(1024)S(1)} %compare_select_fusion, bf16[1,1,64,16,3584]{4,3,2,1,0:T(8,128)(2,1)} %param.8), kind=kLoop, calls=%fused_computation.1 | loop fusion | flops 11010048 | bytes 14684160 | tf_op jit(solution)/shard_map/convert_element_type | solution.py:20
  56.3 3.7 %convolution_convert_fusion.1 = bf16[3584,256]{0,1:T(8,128)(2,1)S(1)} fusion(bf16[1024,3584]{1,0:T(8,128)(2,1)S(1)} %fusion, f32[1024,256]{0,1:T(8,128)} %fusion.7, f32[1024,256]{0,1:T(8,128)} %fusion.4), kind=kOutput, calls=%fused_computation.7 | convolution fusion | flops 1881538560 | bytes 11272192 | tf_op jit(solution)/shard_map/dot_general | solution.py:54
  60.0 7.8 %fusion.1 = bf16[3584,512]{0,1:T(8,128)(2,1)S(1)} fusion(bf16[1024,3584]{1,0:T(8,128)(2,1)} %bitcast.57, bf16[1024,256]{0,1:T(8,128)(2,1)S(1)} %get-tuple-element.23, bf16[1024,256]{0,1:T(8,128)(2,1)S(1)} %get-tuple-element.24), kind=kOutput, calls=%fused_computation.6 | convolution fusion | flops 3762028544 | bytes 12058624 | tf_op jit(solution)/shard_map/dot_general | solution.py:51
  67.8 2.7 %pad_maximum_fusion = bf16[3584,768]{0,1:T(8,128)(2,1)} fusion(bf16[3584,256]{0,1:T(8,128)(2,1)S(1)} %convolution_convert_fusion.1, bf16[3584,512]{0,1:T(8,128)(2,1)S(1)} %fusion.1), kind=kLoop, calls=%fused_computation.5 | loop fusion | flops 11010048 | bytes 11010048 | tf_op jit(solution)/shard_map/concatenate | solution.py:58
  70.5 0.0 reduce-scatter.5.cloned.1.call-update
  70.6 33.2 %reduce-scatter.7.cloned.1.call-done = bf16[8,57344]{1,0:T(8,128)(2,1)} async-done(((bf16[64,57344]{1,0:T(8,128)(2,1)}), bf16[8,57344]{1,0:T(8,128)(2,1)}) %reduce-scatter.7.cloned.1.call-update) | async-done | bytes 917520
  103.8 0.0 copy-start.1
  103.8 9.4 %all-to-all-start = ((bf16[8,16,3584]{2,0,1:T(8,128)(2,1)}), bf16[8,16,3584]{2,0,1:T(8,128)(2,1)S(1)}, u32[]{:S(2)}, u32[]{:S(2)}) async-start(bf16[8,16,3584]{2,0,1:T(8,128)(2,1)} %bitcast.53), calls=%async_computation | async-start | bytes 1835008 | tf_op jit(solution)/shard_map/all_to_all | solution.py:49
  113.2 81.9 %reduce-scatter.5.cloned.1.call-done = bf16[1792,768]{0,1:T(8,128)(2,1)} async-done(((bf16[3584,768]{0,1:T(8,128)(2,1)}), bf16[1792,768]{0,1:T(8,128)(2,1)}) %reduce-scatter.5.cloned.1.call-update) | async-done | bytes 2752528 | tf_op jit(solution)/shard_map/reduce_scatter | solution.py:57
  195.1 3.3 %slice_bitcast_fusion = (bf16[1,1792,256]{1,2,0:T(8,128)(2,1)}, bf16[1,1792,256]{1,2,0:T(8,128)(2,1)}, bf16[1,1792,256]{1,2,0:T(8,128)(2,1)}) fusion(bf16[1792,768]{0,1:T(8,128)(2,1)} %reduce-scatter.5.cloned.1.call-done), kind=kLoop, calls=%fused_computation.25 | loop fusion | bytes 5505024 | tf_op jit(solution)/shard_map/broadcast_in_dim | solution.py:65
  198.4 2.2 %copy.31 = bf16[1,1792,256]{2,1,0:T(8,128)(2,1)} copy(bf16[1,1792,256]{1,2,0:T(8,128)(2,1)} %get-tuple-element.22) | data formatting | bytes 1835008
  200.6 2.2 %copy.32 = bf16[1,1792,256]{2,1,0:T(8,128)(2,1)} copy(bf16[1,1792,256]{1,2,0:T(8,128)(2,1)} %get-tuple-element.21) | data formatting | bytes 1835008
  202.8 2.2 %copy.33 = bf16[1,1792,256]{2,1,0:T(8,128)(2,1)} copy(bf16[1,1792,256]{1,2,0:T(8,128)(2,1)} %get-tuple-element.20) | data formatting | bytes 1835008
  205.1 0.0 all-to-all-done
  205.1 1.2 copy.30
  206.3 0.0 copy-done.1
  (3 shorter events, 0.0 us)
Async XLA Ops:
  7.2 1.5 copy-start
  7.2 96.6 %reduce-scatter.7.cloned.1.call-start = ((), (), s32[]{:S(2)}) async-start(), calls=%async_computation.4 | async-start | bytes 8257536
  8.7 6.3 %copy-start.2 = (bf16[1,3584,256]{2,1,0:T(8,128)(2,1)S(1)}, bf16[1,3584,256]{2,1,0:T(8,128)(2,1)}, u32[]{:S(2)}) copy-start(bf16[1,3584,256]{2,1,0:T(8,128)(2,1)} %param.12) | copy-start | bytes 5505028
  8.7 6.3 %copy-start.6 = (bf16[1,1,64,16,3584]{4,3,2,1,0:T(8,128)(2,1)S(1)}, bf16[1,1,64,16,3584]{4,3,2,1,0:T(8,128)(2,1)}, u32[]{:S(2)}) copy-start(bf16[1,1,64,16,3584]{4,3,2,1,0:T(8,128)(2,1)} %param.7) | copy-start | bytes 22020100
  15.0 3.1 %copy-start.4 = (f32[1,1,64,16]{2,3,1,0:T(8,128)S(1)}, f32[1,1,64,16]{2,3,1,0:T(8,128)}, u32[]{:S(2)}) copy-start(f32[1,1,64,16]{2,3,1,0:T(8,128)} %param.9) | copy-start | bytes 12292
  15.0 3.1 %copy-start.5 = (s32[1,1,16]{2,1,0:T(1,128)S(1)}, s32[1,1,16]{2,1,0:T(1,128)}, u32[]{:S(2)}) copy-start(s32[1,1,16]{2,1,0:T(1,128)} %param.10) | copy-start | bytes 196
  28.3 7.3 %copy-start.3 = (bf16[1,3584,256]{2,1,0:T(8,128)(2,1)S(1)}, bf16[1,3584,256]{2,1,0:T(8,128)(2,1)}, u32[]{:S(2)}) copy-start(bf16[1,3584,256]{2,1,0:T(8,128)(2,1)} %param.12) | copy-start | bytes 5505028
  50.4 144.7 %reduce-scatter.5.cloned.1.call-start = ((), (), s32[]{:S(2)}) async-start(), calls=%async_computation.3 | async-start | bytes 8257536 | tf_op jit(solution)/shard_map/reduce_scatter | solution.py:57
  103.8 102.5 %copy-start.1 = (bf16[1,3584,256]{2,1,0:T(8,128)(2,1)S(1)}, bf16[1,3584,256]{2,1,0:T(8,128)(2,1)}, u32[]{:S(2)}) copy-start(bf16[1,3584,256]{2,1,0:T(8,128)(2,1)} %param.11) | copy-start | bytes 5505028
  103.8 101.3 %all-to-all-start = ((bf16[8,16,3584]{2,0,1:T(8,128)(2,1)}), bf16[8,16,3584]{2,0,1:T(8,128)(2,1)S(1)}, u32[]{:S(2)}, u32[]{:S(2)}) async-start(bf16[8,16,3584]{2,0,1:T(8,128)(2,1)} %bitcast.53), calls=%async_computation | async-start | bytes 1835008 | tf_op jit(solution)/shard_map/all_to_all | solution.py:49
Sparse Core Ops, SparseCore 0:
  50.5 53.2 reduce-scatter.6
  106.3 88.7 reduce-scatter.4
where the time goes:
time: 214 us; the launch traced here: 213 us
  waiting for transfers between devices  115 us (54%)
  matrix products  40.2 us (19%)
  local copies, waits for them, and re-layouts  20.2 us (9%)
  between operations  14.1 us (7%)
  other arithmetic  13.9 us (6%)
  starting transfers between devices  9.47 us (4%)
    reduce_scatter x1, waiting for transfers between devices, on_device(): lax.psum_scatter(jnp.concatenate((front, behind), axis=1).astype(jnp.bflo...  81.9 us
    unnamed x3, waiting for transfers between devices  33.2 us
    unnamed x20, local copies, waits for them, and re-layouts  16.5 us
    convert_element_type x2, other arithmetic, on_device(): scaled_rows = (grad_rows[0, 0].astype(jnp.float32) * (combine_weights[0,...  11.1 us
    all_to_all x1, starting transfers between devices, on_device(): lax.all_to_all(summed, 'node', split_axis=1, concat_axis=1, tiled=True)  9.39 us
    dot_general x1, matrix products, on_device(): lax.dot_general(flat_tokens, joined_grad, (((0,), (0,)), ((), ())), prefe...  7.78 us
    dot_general x1, matrix products, on_device(): lax.dot_general(up_grad, up_weight, (((1,), (1,)), ((), ())), preferred_e...  7.51 us
    dot_general x1, matrix products, on_device(): lax.dot_general(gate_grad, gate_weight, (((1,), (1,)), ((), ())), preferr...  7.33 us
  transfers between devices with their start and end apart: 3, of which 2 were waited for; matrix products, arithmetic and copies ran while one was open for 14% of the time, Pallas kernels for 0%

commit v1 on v0

--- a/solution.py
+++ b/solution.py
@@ -2,6 +2,12 @@
 import jax.numpy as jnp
 from jax import lax
 from jax.sharding import PartitionSpec as P
+
+
+def trade_parts(x, axis, split, join):
+    shards = jnp.split(x, lax.axis_size(axis), axis=split)
+    received = lax.all_to_all(jnp.stack(shards), axis, 0, 0)
+    return jnp.concatenate(received, axis=join)
 
 
 def on_device(tokens_in, grad_rows, combine_weights, live_counts, w_gate, w_up, w_down):
@@ -46,7 +52,7 @@
         scatter_dimension=0,
         tiled=True,
     )
-    returned = lax.all_to_all(summed, "node", split_axis=1, concat_axis=1, tiled=True)
+    returned = trade_parts(summed, "node", 1, 1)
     d_tokens = returned[None, None]
     front = lax.dot_general(
         flat_tokens, joined_grad, (((0,), (0,)), ((), ())), preferred_element_type=jnp.float32

time: 214 us -> 219 us (1.023)
  local copies, waits for them, and re-layouts: 20.2 us -> 43.4 us
  waiting for transfers between devices: 115 us -> 96.8 us
    unnamed x20 -> x35, local copies, waits for them, and re-layouts: 16.5 us -> 38.2 us
    reduce_scatter x1, waiting for transfers between devices: 81.9 us -> 63.6 us  [on_device(): lax.psum_scatter(jnp.concatenate((front, behind), axis=1).astype(jnp.bflo...]
  transfers between devices with their start and end apart: 3 -> 3, of which waited for: 2 -> 2; matrix products, arithmetic and copies ran while one was open for 14% -> 24% of each run, Pallas kernels for 0% -> 0%
where the time goes in v1:
time: 219 us; the launch traced here: 218 us
  waiting for transfers between devices  96.8 us (44%)
  local copies, waits for them, and re-layouts  43.4 us (20%)
  matrix products  40.2 us (18%)
  between operations  14.1 us (6%)
  other arithmetic  13.9 us (6%)
  starting transfers between devices  9.34 us (4%)
    reduce_scatter x1, waiting for transfers between devices, on_device(): lax.psum_scatter(jnp.concatenate((front, behind), axis=1).astype(jnp.bflo...  63.6 us
    unnamed x35, local copies, waits for them, and re-layouts  38.2 us
    unnamed x3, waiting for transfers between devices  33.3 us
    convert_element_type x2, other arithmetic, on_device(): scaled_rows = (grad_rows[0, 0].astype(jnp.float32) * (combine_weights[0,...  11.1 us
    all_to_all x1, starting transfers between devices, trade_parts(): received = lax.all_to_all(jnp.stack(shards), axis, 0, 0)  9.26 us
    dot_general x1, matrix products, on_device(): lax.dot_general(flat_tokens, joined_grad, (((0,), (0,)), ((), ())), prefe...  7.74 us
    dot_general x1, matrix products, on_device(): lax.dot_general(up_grad, up_weight, (((1,), (1,)), ((), ())), preferred_e...  7.51 us
    dot_general x1, matrix products, on_device(): lax.dot_general(gate_grad, gate_weight, (((1,), (1,)), ((), ())), preferr...  7.33 us
  transfers between devices with their start and end apart: 3, of which 2 were waited for; matrix products, arithmetic and copies ran while one was open for 24% of the time, Pallas kernels for 0%

profile of v1, /device:TPU:1, one launch (start us, length us, event | category | flops | bytes accessed | tf_op | source)
XLA Modules:
  0.0 217.9 jit_solution(16130116428871042441)
XLA Ops:
  7.2 0.0 copy-start
  7.2 0.0 reduce-scatter.7.cloned.1.call-start
  7.2 1.4 copy-done
  8.7 6.3 %fusion.4 = f32[1024,256]{0,1:T(8,128)} fusion(bf16[1024,3584]{1,0:T(8,128)(2,1)} %bitcast.137, bf16[1,3584,256]{2,1,0:T(8,128)(2,1)S(1)} %copy-done), kind=kOutput, calls=%fused_computation.10 | convolution fusion | flops 1879048192 | bytes 10223616 | tf_op jit(solution)/shard_map/dot_general | solution.py:29
  15.0 3.1 %fusion.7 = f32[1024,256]{0,1:T(8,128)} fusion(bf16[1024,3584]{1,0:T(8,128)(2,1)S(1)} %bitcast.139, bf16[1,3584,256]{2,1,0:T(8,128)(2,1)S(1)} %copy-done.2), kind=kOutput, calls=%fused_computation.13 | convolution fusion | flops 1879048192 | bytes 10223616 | tf_op jit(solution)/shard_map/dot_general | solution.py:30
  18.1 0.1 bitcast_select_fusion
  18.2 0.1 copy.38
  18.2 5.6 %multiply_convert_fusion = bf16[1,1,64,16,3584]{4,3,2,1,0:T(8,128)(2,1)S(1)} fusion(f32[64,16]{1,0:T(8,128)S(1)} %copy.38, bf16[1,1,64,16,3584]{4,3,2,1,0:T(8,128)(2,1)} %param.8), kind=kLoop, calls=%fused_computation.3 | loop fusion | flops 11010048 | bytes 14684160 | tf_op jit(solution)/shard_map/convert_element_type | solution.py:26
  23.8 4.5 %multiply_convert_fusion.2 = (bf16[1024,256]{0,1:T(8,128)(2,1)S(1)}, bf16[1024,256]{0,1:T(8,128)(2,1)S(1)}) fusion(f32[1024,256]{0,1:T(8,128)} %fusion.4, f32[1024,256]{0,1:T(8,128)} %fusion.7, bf16[1024,3584]{1,0:T(8,128)(2,1)S(1)} %bitcast.117, bf16[1,3584,256]{2,1,0:T(8,128)(2,1)} %param.13), kind=kOutput, calls=%fused_computation.21 | convolution fusion | flops 1882456064 | bytes 12320768 | tf_op jit(solution)/shard_map/dot_general | solution.py:34
  28.3 0.0 copy-start.3
  28.4 7.3 %fusion.2 = f32[1024,3584]{1,0:T(8,128)} fusion(bf16[1024,256]{0,1:T(8,128)(2,1)S(1)} %get-tuple-element.20, bf16[1,3584,256]{2,1,0:T(8,128)(2,1)S(1)} %copy-done), kind=kOutput, calls=%fused_computation.8 | convolution fusion | flops 1879048192 | bytes 17039360 | tf_op jit(solution)/shard_map/dot_general | solution.py:41
  35.7 7.5 %add_convert_fusion = bf16[1024,3584]{1,0:T(8,128)(2,1)S(1)} fusion(f32[1024,3584]{1,0:T(8,128)} %fusion.2, bf16[1024,256]{0,1:T(8,128)(2,1)S(1)} %get-tuple-element.19, bf16[1,3584,256]{2,1,0:T(8,128)(2,1)S(1)} %copy-done.3), kind=kOutput, calls=%fused_computation.2 | convolution fusion | flops 1886388224 | bytes 24379392 | tf_op jit(solution)/shard_map/dot_general | solution.py:44
  43.2 7.1 %copy.47 = bf16[8,8,16,3584]{3,1,2,0:T(8,128)(2,1)} copy(bf16[8,8,16,3584]{3,2,1,0:T(8,128)(2,1)S(1)} %bitcast.116) | data formatting | bytes 14680064
  50.4 0.0 reduce-scatter.7.cloned.1.call-update
  50.4 0.0 reduce-scatter.5.cloned.1.call-start
  50.4 0.1 copy.40
  50.5 0.1 lt.25
  50.6 0.1 iota.15
  50.7 0.1 squeeze.19
  50.8 5.5 %fusion = bf16[1024,3584]{1,0:T(8,128)(2,1)S(1)} fusion(f32[1024]{0:T(1024)S(1)} %compare_select_fusion, bf16[1,1,64,16,3584]{4,3,2,1,0:T(8,128)(2,1)} %param.8), kind=kLoop, calls=%fused_computation.1 | loop fusion | flops 11010048 | bytes 14684160 | tf_op jit(solution)/shard_map/convert_element_type | solution.py:26
  56.3 3.7 %convolution_convert_fusion.1 = bf16[3584,256]{0,1:T(8,128)(2,1)S(1)} fusion(bf16[1024,3584]{1,0:T(8,128)(2,1)S(1)} %fusion, f32[1024,256]{0,1:T(8,128)} %fusion.7, f32[1024,256]{0,1:T(8,128)} %fusion.4), kind=kOutput, calls=%fused_computation.7 | convolution fusion | flops 1881538560 | bytes 11272192 | tf_op jit(solution)/shard_map/dot_general | solution.py:60
  60.0 7.7 %fusion.1 = bf16[3584,512]{0,1:T(8,128)(2,1)S(1)} fusion(bf16[1024,3584]{1,0:T(8,128)(2,1)} %bitcast.138, bf16[1024,256]{0,1:T(8,128)(2,1)S(1)} %get-tuple-element.19, bf16[1024,256]{0,1:T(8,128)(2,1)S(1)} %get-tuple-element.20), kind=kOutput, calls=%fused_computation.6 | convolution fusion | flops 3762028544 | bytes 12058624 | tf_op jit(solution)/shard_map/dot_general | solution.py:57
  67.8 2.7 %pad_maximum_fusion = bf16[3584,768]{0,1:T(8,128)(2,1)} fusion(bf16[3584,256]{0,1:T(8,128)(2,1)S(1)} %convolution_convert_fusion.1, bf16[3584,512]{0,1:T(8,128)(2,1)S(1)} %fusion.1), kind=kLoop, calls=%fused_computation.5 | loop fusion | flops 11010048 | bytes 11010048 | tf_op jit(solution)/shard_map/concatenate | solution.py:64
  70.5 0.0 reduce-scatter.5.cloned.1.call-update
  70.5 33.2 %reduce-scatter.7.cloned.1.call-done = bf16[8,57344]{1,0:T(8,128)(2,1)} async-done(((bf16[64,57344]{1,0:T(8,128)(2,1)}), bf16[8,57344]{1,0:T(8,128)(2,1)}) %reduce-scatter.7.cloned.1.call-update) | async-done | bytes 917520
  103.8 1.4 fusion.31
  105.2 1.4 fusion.30
  106.7 1.4 fusion.29
  108.1 1.4 fusion.28
  109.6 1.4 fusion.27
  111.0 1.4 fusion.26
  112.4 1.4 fusion.25
  113.9 1.4 fusion.24
  115.3 1.4 fusion.23
  116.8 1.4 fusion.22
  118.2 1.5 fusion.21
  119.7 1.4 fusion.20
  121.1 1.4 fusion.19
  122.6 1.4 fusion.18
  124.0 1.4 fusion.17
  125.5 1.6 fusion.16
  127.0 9.3 %all-to-all-start = ((bf16[16,8,1,3584]{3,1,2,0:T(8,128)(2,1)}), bf16[16,8,1,3584]{3,1,2,0:T(8,128)(2,1)S(1)}, u32[]{:S(2)}, u32[]{:S(2)}) async-start(bf16[16,8,1,3584]{3,1,2,0:T(8,128)(2,1)} %fusion.16), calls=%async_computation | async-start | bytes 1835008 | tf_op jit(solution)/shard_map/all_to_all | solution.py:9
  136.3 63.6 %reduce-scatter.5.cloned.1.call-done = bf16[1792,768]{0,1:T(8,128)(2,1)} async-done(((bf16[3584,768]{0,1:T(8,128)(2,1)}), bf16[1792,768]{0,1:T(8,128)(2,1)}) %reduce-scatter.5.cloned.1.call-update) | async-done | bytes 2752528 | tf_op jit(solution)/shard_map/reduce_scatter | solution.py:63
  199.9 3.3 %slice_bitcast_fusion = (bf16[1,1792,256]{1,2,0:T(8,128)(2,1)}, bf16[1,1792,256]{1,2,0:T(8,128)(2,1)}, bf16[1,1792,256]{1,2,0:T(8,128)(2,1)}) fusion(bf16[1792,768]{0,1:T(8,128)(2,1)} %reduce-scatter.5.cloned.1.call-done), kind=kLoop, calls=%fused_computation.25 | loop fusion | bytes 5505024 | tf_op jit(solution)/shard_map/broadcast_in_dim | solution.py:71
  203.2 2.2 %copy.42 = bf16[1,1792,256]{2,1,0:T(8,128)(2,1)} copy(bf16[1,1792,256]{1,2,0:T(8,128)(2,1)} %get-tuple-element.18) | data formatting | bytes 1835008
  205.4 2.2 %copy.43 = bf16[1,1792,256]{2,1,0:T(8,128)(2,1)} copy(bf16[1,1792,256]{1,2,0:T(8,128)(2,1)} %get-tuple-element.17) | data formatting | bytes 1835008
  207.6 2.2 %copy.44 = bf16[1,1792,256]{2,1,0:T(8,128)(2,1)} copy(bf16[1,1792,256]{1,2,0:T(8,128)(2,1)} %get-tuple-element.16) | data formatting | bytes 1835008
  209.8 1.2 copy.41
  (15 shorter events, 0.0 us)
Async XLA Ops:
  7.2 1.5 copy-start
  7.2 96.6 %reduce-scatter.7.cloned.1.call-start = ((), (), s32[]{:S(2)}) async-start(), calls=%async_computation.4 | async-start | bytes 8257536
  8.7 6.3 %copy-start.2 = (bf16[1,3584,256]{2,1,0:T(8,128)(2,1)S(1)}, bf16[1,3584,256]{2,1,0:T(8,128)(2,1)}, u32[]{:S(2)}) copy-start(bf16[1,3584,256]{2,1,0:T(8,128)(2,1)} %param.12) | copy-start | bytes 5505028
  8.7 6.3 %copy-start.6 = (bf16[1,1,64,16,3584]{4,3,2,1,0:T(8,128)(2,1)S(1)}, bf16[1,1,64,16,3584]{4,3,2,1,0:T(8,128)(2,1)}, u32[]{:S(2)}) copy-start(bf16[1,1,64,16,3584]{4,3,2,1,0:T(8,128)(2,1)} %param.7) | copy-start | bytes 22020100
  15.0 3.1 %copy-start.4 = (f32[1,1,64,16]{2,3,1,0:T(8,128)S(1)}, f32[1,1,64,16]{2,3,1,0:T(8,128)}, u32[]{:S(2)}) copy-start(f32[1,1,64,16]{2,3,1,0:T(8,128)} %param.9) | copy-start | bytes 12292
  15.0 3.1 %copy-start.5 = (s32[1,1,16]{2,1,0:T(1,128)S(1)}, s32[1,1,16]{2,1,0:T(1,128)}, u32[]{:S(2)}) copy-start(s32[1,1,16]{2,1,0:T(1,128)} %param.10) | copy-start | bytes 196
  28.3 7.3 %copy-start.3 = (bf16[1,3584,256]{2,1,0:T(8,128)(2,1)S(1)}, bf16[1,3584,256]{2,1,0:T(8,128)(2,1)}, u32[]{:S(2)}) copy-start(bf16[1,3584,256]{2,1,0:T(8,128)(2,1)} %param.12) | copy-start | bytes 5505028
  50.4 149.5 %reduce-scatter.5.cloned.1.call-start = ((), (), s32[]{:S(2)}) async-start(), calls=%async_computation.3 | async-start | bytes 8257536 | tf_op jit(solution)/shard_map/reduce_scatter | solution.py:63
  125.5 85.6 %copy-start.1 = (bf16[1,3584,256]{2,1,0:T(8,128)(2,1)S(1)}, bf16[1,3584,256]{2,1,0:T(8,128)(2,1)}, u32[]{:S(2)}) copy-start(bf16[1,3584,256]{2,1,0:T(8,128)(2,1)} %param.11) | copy-start | bytes 5505028
  127.0 82.8 %all-to-all-start = ((bf16[16,8,1,3584]{3,1,2,0:T(8,128)(2,1)}), bf16[16,8,1,3584]{3,1,2,0:T(8,128)(2,1)S(1)}, u32[]{:S(2)}, u32[]{:S(2)}) async-start(bf16[16,8,1,3584]{3,1,2,0:T(8,128)(2,1)} %fusion.16), calls=%async_computation | async-start | bytes 1835008 | tf_op jit(solution)/shard_map/all_to_all | solution.py:9
Sparse Core Ops, SparseCore 0:
  50.5 53.2 reduce-scatter.6
  106.3 93.4 reduce-scatter.4
